TPU v7x, 256 devices: a whole 4x4x8 slice. The times are simulated.
256 devices in a mesh: cells: 64 (over z, x, core), chan: 4 (over y).
Axes of the slice: x: 4, y: 4, z: 8, core: 2. Of those that a mesh axis runs over, the one named last changes fastest.
Arguments:
- charges: bfloat16 [128, 65536], P('chan', 'cells'), may hold values from -6 to 6
- basis: float32 [25, 65536], P(None, 'cells'), may hold values from -1.5 to 1.5
- atom_leaf: int32 [65536], P('cells'), may hold values from 0 to 8191, as said below
- leaf_lists: int32 [64, 8192], P(None, 'cells'), may hold values from -1 to 8191, as said below
- coarse_lists: int32 [64, 1024], P(None, 'cells'), may hold values from -1 to 1023, as said below
- up_ops: bfloat16 [8, 25, 25], replicated, may hold values from -0.4375 to 0.4375
- down_ops: bfloat16 [8, 25, 25], replicated, may hold values from -1.25 to 1.25
- leaf_ops: bfloat16 [25, 25, 64], replicated, may hold values from -0.15625 to 0.15625
- coarse_ops: bfloat16 [25, 25, 64], replicated, may hold values from -0.15625 to 0.15625
- mix: bfloat16 [128, 128], replicated, may hold values from -0.5 to 0.5
- cotangent: bfloat16 [128, 65536], P('chan', 'cells'), may hold values from -0.005859375 to 0.005859375
Outputs:
- refined: bfloat16 [128, 65536], P('chan', 'cells')
- grad_leaf_ops: float32 [25, 25, 64], replicated
- grad_coarse_ops: float32 [25, 25, 64], replicated
Inputs may be any that keep to these rules, and one draw needn't show every extreme that they name: `atom_leaf`: an atom's leaf is one of the 128 consecutive leaves whose block along cells holds that atom. `leaf_lists`: entry [s, t] is -1 for an empty slot, else a leaf within 64 leaves of the block of 128 leaves that holds t. `coarse_lists`: entry [s, p] is -1 for an empty slot, else a parent cell within 8 cells of the block of 16 parent cells that holds p.
All inputs are finite; a program needn't handle non-finite values.
Results may differ from a plain program's by a relative error of at most 0.014.
Values may be sent and summed in bfloat16 or wider, within the bound.
A program may use at most 128 MiB of HBM per device.

v0:
```python
import jax
import jax.numpy as jnp
from jax import lax
from jax.sharding import PartitionSpec as P

SLOT_BLOCK = 16


def extended(block, sides, width):
    for axis, dim in sides:
        count = lax.axis_size(axis)
        forward = [(i, i + 1) for i in range(count - 1)]
        backward = [(target, source) for source, target in forward]
        low = lax.ppermute(
            lax.slice_in_dim(block, block.shape[dim] - width, None, axis=dim), axis, forward
        )
        high = lax.ppermute(lax.slice_in_dim(block, 0, width, axis=dim), axis, backward)
        block = jnp.concatenate([low, block, high], axis=dim)
    return block


def spread(weights, values, local_leaf, leaf_dev):
    kcount, atoms = weights.shape
    chan_part = values.shape[0]
    width = min(1024, atoms)

    def spread_accumulate(counter, running):
        member = (local_leaf[:, None] == jnp.arange(leaf_dev, dtype=jnp.int32)[None, :]).astype(
            jnp.bfloat16
        )
        scaled = (weights[:, None, :] * values[None].astype(jnp.float32)).astype(jnp.bfloat16)
        return running + jnp.dot(
            scaled.reshape(kcount * chan_part, width), member, preferred_element_type=jnp.float32
        )

    start_value = jnp.zeros((kcount * chan_part, leaf_dev), jnp.float32)
    result = lax.fori_loop(0, atoms // width, spread_accumulate, start_value)
    return result.reshape(kcount, chan_part, leaf_dev)


def collect(weights, fields, local_leaf):
    kcount, chan_part, leaf_dev = fields.shape
    atoms = weights.shape[1]
    width = min(1024, atoms)
    flat_fields = fields.reshape(kcount * chan_part, leaf_dev)

    def collect_accumulate(counter, running):
        member = (jnp.arange(leaf_dev, dtype=jnp.int32)[:, None] == local_leaf[None, :]).astype(
            jnp.bfloat16
        )
        per_atom = jnp.dot(flat_fields, member, preferred_element_type=jnp.float32).reshape(
            kcount, chan_part, width
        )
        summed = jnp.sum(weights[:, None, :] * per_atom, axis=0)
        return summed

    start_value = jnp.zeros((chan_part, atoms), jnp.float32)
    return lax.fori_loop(0, atoms // width, collect_accumulate, start_value)


def pick(source, group_list, first_cell):
    valid = group_list >= 0
    position = jnp.where(valid, group_list - first_cell, 0)
    picked = jnp.take(source, position, axis=2)
    return picked * valid.astype(jnp.bfloat16)[None, None]


def translate(source, lists, first_cell, ops):
    kcount, chan_part, _ = source.shape
    slot_count, targets = lists.shape
    groups = slot_count // SLOT_BLOCK
    list_groups = lists.reshape(groups, SLOT_BLOCK, targets)
    op_groups = jnp.transpose(ops.reshape(kcount, kcount, groups, SLOT_BLOCK), (2, 3, 0, 1))

    def translate_advance(running, pieces):
        group_list, group_ops = pieces
        picked = pick(source, group_list, first_cell)
        return (
            running
            + jnp.einsum("okj,jcot->kct", group_ops, picked, preferred_element_type=jnp.float32),
            None,
        )

    start_value = jnp.zeros((kcount, chan_part, targets), jnp.float32)
    result, _ = lax.scan(translate_advance, start_value, (list_groups, op_groups))
    return result


def slot_gradients(source, lists, first_cell, fields):
    kcount = source.shape[0]
    slot_count, targets = lists.shape
    groups = slot_count // SLOT_BLOCK
    list_groups = lists.reshape(groups, SLOT_BLOCK, targets)

    def slot_advance(carried, group_list):
        picked = pick(source, group_list, first_cell)
        return (
            carried,
            jnp.einsum("kct,jcot->kjo", fields, picked, preferred_element_type=jnp.float32),
        )

    _, stacked = lax.scan(slot_advance, jnp.zeros((), jnp.float32), list_groups)
    return jnp.transpose(stacked, (1, 2, 0, 3)).reshape(kcount, kcount, slot_count)


def local(
    charges,
    basis,
    atom_leaf,
    leaf_lists,
    coarse_lists,
    up_ops,
    down_ops,
    leaf_ops,
    coarse_ops,
    mix,
    cotangent,
):
    chan_part = charges.shape[0]
    kcount = basis.shape[0]
    leaf_dev = leaf_lists.shape[1]
    coarse_dev = coarse_lists.shape[1]
    cells_pos = lax.axis_index("cells")
    chan_pos = lax.axis_index("chan")
    local_leaf = atom_leaf - cells_pos * leaf_dev
    moments = spread(basis, charges, local_leaf, leaf_dev).astype(jnp.bfloat16)
    grouped = moments.reshape(kcount, chan_part, coarse_dev, 8)
    coarse = jnp.einsum(
        "okj,jcpo->kcp", up_ops, grouped, preferred_element_type=jnp.float32
    ).astype(jnp.bfloat16)
    leaf_source = extended(moments, (("cells", 2),), leaf_dev // 2)
    leaf_first = cells_pos * leaf_dev - leaf_dev // 2
    coarse_source = extended(coarse, (("cells", 2),), coarse_dev // 2)
    coarse_first = cells_pos * coarse_dev - coarse_dev // 2
    near_field = translate(leaf_source, leaf_lists, leaf_first, leaf_ops)
    far_field = translate(coarse_source, coarse_lists, coarse_first, coarse_ops).astype(
        jnp.bfloat16
    )
    child = jnp.einsum("okj,jcp->kcpo", down_ops, far_field, preferred_element_type=jnp.float32)
    expansion = (near_field + child.reshape(kcount, chan_part, leaf_dev)).astype(jnp.bfloat16)
    potential = collect(basis, expansion, local_leaf).astype(jnp.bfloat16)
    rows_mine = lax.dynamic_slice_in_dim(mix, chan_pos * chan_part, chan_part, 0)
    cols_mine = lax.dynamic_slice_in_dim(mix, chan_pos * chan_part, chan_part, 1)
    mixed = lax.dot_general(
        cols_mine,
        lax.all_gather(potential, "chan", axis=0, tiled=True),
        (((0,), (0,)), ((), ())),
        preferred_element_type=jnp.float32,
    )
    back_sum = jnp.dot(
        rows_mine,
        lax.all_gather(cotangent, "chan", axis=0, tiled=True),
        preferred_element_type=jnp.float32,
    )
    refined = (charges.astype(jnp.float32) + mixed).astype(jnp.bfloat16)
    back_potential = back_sum.astype(jnp.bfloat16)
    back_expansion = spread(basis, back_potential, local_leaf, leaf_dev).astype(jnp.bfloat16)
    back_grouped = back_expansion.reshape(kcount, chan_part, coarse_dev, 8)
    back_far = jnp.einsum(
        "okj,kcpo->jcp", down_ops, back_grouped, preferred_element_type=jnp.float32
    ).astype(jnp.bfloat16)
    grad_leaf = slot_gradients(leaf_source, leaf_lists, leaf_first, back_expansion)
    grad_coarse = slot_gradients(coarse_source, coarse_lists, coarse_first, back_far)
    grad_leaf, grad_coarse = lax.psum((grad_leaf, grad_coarse), ("cells", "chan"))
    return (refined, grad_leaf, grad_coarse)


def solution(mesh):
    placed = (
        P("chan", "cells"),
        P(None, "cells"),
        P("cells"),
        P(None, "cells"),
        P(None, "cells"),
        P(),
        P(),
        P(),
        P(),
        P(),
        P("chan", "cells"),
    )
    return jax.shard_map(
        local, mesh=mesh, in_specs=placed, out_specs=(P("chan", "cells"), P(), P()), check_vma=False
    )
```

profile of v0, /device:TPU:2, one launch (start us, length us, event | category | flops | bytes accessed | tf_op | source)
XLA Modules:
  0.0 724.2 jit_solution(9109661945923828574)
XLA Ops:
  17.7 3.8 collective-permute-start.3
  23.4 12.3 %all_gather.7 = bf16[128,1024]{1,0:T(8,128)(2,1)S(1)} all-gather(bf16[32,1024]{1,0:T(8,128)(2,1)S(1)} %copy-done.9), channel_id=1, replica_groups=mesh['cells'=64,'chan'=4] {'chan'}, dimensions={0}, use_global_device_ids=true | all-gather | bytes 327680 | tf_op jit(solution)/shard_map/all_gather | solution.py:152
  43.4 13.1 %while.57 = (s32[]{:T(128)}, f32[25,32,16]{1,0,2:T(8,128)S(1)}, bf16[4,16,25,25]{3,2,1,0:T(8,128)(2,1)S(1)}, s32[4,16,16]{2,1,0:T(8,128)S(1)}, s32[]{:T(128)}, /...) while((s32[]{:T(128)}, f32[25,32,16]{1,0,2:T(8,128)S(1)}, ...), condition=%wide.region_3.6_spmd.clone, body=%wide.region_2.5_spmd.clone.sunk | while | flops 10678787 | bytes 4553847 | solution.py:85
  56.6 17.5 %while.15 = (s32[]{:T(128)}, f32[4,25,25,16]{1,2,3,0:T(8,128)}, s32[4,16,16]{2,1,0:T(8,128)S(1)}, s32[]{:T(128)}, bf16[25,32,32]{1,0,2:T(8,128)(2,1)S(1)}, /*index=5*/bf16[25,32,16]{1,0,2:T(8,128)(2,1)}, s32[]{:T(128)}) while((s32[]{:T(128)}, f32[4,25,25,16]{1,2,3,0:T(8,128)}, s32[4,16,16]{2,1,0:T(8,128)S(1)}, s32[]{:T(128)}, ...), condition=%wide.region_9.12_spmd, body=%wide.region_8.11_spmd.sunk | while | flops 10653186 | bytes 3270785 | solution.py:102
  83.2 193.7 %while.56 = (s32[]{:T(128)}, f32[25,32,128]{2,0,1:T(8,128)}, bf16[4,16,25,25]{3,2,1,0:T(8,128)(2,1)}, s32[4,16,128]{2,1,0:T(8,128)S(1)}, s32[]{:T(128)}, /*index...) while((s32[]{:T(128)}, f32[25,32,128]{2,0,1:T(8,128)}, bf16[4,16,25,25]{3,2,1,0:T(8,128)(2,1)}, ...), condition=%wide.region_1.3_spmd.clone, body=%wide.region_0.2_spmd.clone.sunk | while | flops 90349568 | bytes 18425984 | solution.py:85
  83.2 19.3 %gather_fusion.2 = bf16[2048,25,32]{2,1,0:T(8,128)(2,1)} fusion(bf16[25,32,256]{1,0,2:T(8,128)(2,1)S(1)} %get-tuple-element.527, s32[2048]{0:T(1024)S(1)} %bitcast_clamp_fusion.5), kind=kCustom, calls=%fused_computation.clone.clone.1 | custom fusion | bytes 6561792 | tf_op jit(solution)/shard_map/while/body/eval_jaxpr/jit(_take)/gather | solution.py:64
  102.5 24.5 %copy.113 = bf16[16,128,25,32]{1,2,0,3:T(8,128)(2,1)} copy(bf16[16,128,25,32]{3,2,1,0:T(8,128)(2,1)} %bitcast.208) | data formatting | bytes 6553600 | tf_op jit(solution)/shard_map/while/body/eval_jaxpr/jit(_take)/gather | solution.py:64
  127.1 4.5 fusion.98
  131.5 19.3 %gather_fusion.2 = bf16[2048,25,32]{2,1,0:T(8,128)(2,1)} fusion(bf16[25,32,256]{1,0,2:T(8,128)(2,1)S(1)} %get-tuple-element.527, s32[2048]{0:T(1024)S(1)} %bitcast_clamp_fusion.5), kind=kCustom, calls=%fused_computation.clone.clone.1 | custom fusion | bytes 6561792 | tf_op jit(solution)/shard_map/while/body/eval_jaxpr/jit(_take)/gather | solution.py:64
  150.8 24.5 %copy.113 = bf16[16,128,25,32]{1,2,0,3:T(8,128)(2,1)} copy(bf16[16,128,25,32]{3,2,1,0:T(8,128)(2,1)} %bitcast.208) | data formatting | bytes 6553600 | tf_op jit(solution)/shard_map/while/body/eval_jaxpr/jit(_take)/gather | solution.py:64
  175.4 4.6 fusion.98
  180.0 19.3 %gather_fusion.2 = bf16[2048,25,32]{2,1,0:T(8,128)(2,1)} fusion(bf16[25,32,256]{1,0,2:T(8,128)(2,1)S(1)} %get-tuple-element.527, s32[2048]{0:T(1024)S(1)} %bitcast_clamp_fusion.5), kind=kCustom, calls=%fused_computation.clone.clone.1 | custom fusion | bytes 6561792 | tf_op jit(solution)/shard_map/while/body/eval_jaxpr/jit(_take)/gather | solution.py:64
  199.3 24.5 %copy.113 = bf16[16,128,25,32]{1,2,0,3:T(8,128)(2,1)} copy(bf16[16,128,25,32]{3,2,1,0:T(8,128)(2,1)} %bitcast.208) | data formatting | bytes 6553600 | tf_op jit(solution)/shard_map/while/body/eval_jaxpr/jit(_take)/gather | solution.py:64
  223.8 4.6 fusion.98
  228.4 19.3 %gather_fusion.2 = bf16[2048,25,32]{2,1,0:T(8,128)(2,1)} fusion(bf16[25,32,256]{1,0,2:T(8,128)(2,1)S(1)} %get-tuple-element.527, s32[2048]{0:T(1024)S(1)} %bitcast_clamp_fusion.5), kind=kCustom, calls=%fused_computation.clone.clone.1 | custom fusion | bytes 6561792 | tf_op jit(solution)/shard_map/while/body/eval_jaxpr/jit(_take)/gather | solution.py:64
  247.7 24.5 %copy.113 = bf16[16,128,25,32]{1,2,0,3:T(8,128)(2,1)} copy(bf16[16,128,25,32]{3,2,1,0:T(8,128)(2,1)} %bitcast.208) | data formatting | bytes 6553600 | tf_op jit(solution)/shard_map/while/body/eval_jaxpr/jit(_take)/gather | solution.py:64
  272.2 4.6 fusion.98
  278.6 12.3 %all_gather.6 = bf16[128,1024]{1,0:T(8,128)(2,1)S(1)} all-gather(bf16[32,1024]{1,0:T(8,128)(2,1)S(1)} %multiply_reduce_fusion), channel_id=1, replica_groups=mesh['cells'=64,'chan'=4] {'chan'}, dimensions={0}, use_global_device_ids=true | all-gather | bytes 327680 | tf_op jit(solution)/shard_map/all_gather | solution.py:146
  290.9 151.2 %while.14 = (s32[]{:T(128)}, f32[4,25,25,16]{1,3,2,0:T(8,128)}, s32[4,16,128]{2,1,0:T(8,128)S(1)}, s32[]{:T(128)}, bf16[25,32,256]{1,0,2:T(8,128)(2,1)S(1)}, /*index=5*/bf16[25,32,128]{2,0,1:T(8,128)(2,1)S(1)}, s32[]{:T(128)}) while((s32[]{:T(128)}, f32[4,25,25,16]{1,3,2,0:T(8,128)}, s32[4,16,128]{2,1,0:T(8,128)S(1)}, s32[]{:T(128)}, ...), condition=%wide.region_6.9_spmd, body=%wide.region_5.8_spmd.sunk | while | flops 85229568 | bytes 16853100 | solution.py:102
  290.9 19.3 %gather_fusion = bf16[2048,25,32]{2,1,0:T(8,128)(2,1)} fusion(bf16[25,32,256]{1,0,2:T(8,128)(2,1)S(1)} %get-tuple-element.572, s32[2048]{0:T(1024)S(1)} %bitcast_clamp_fusion.4), kind=kCustom, calls=%fused_computation.2.clone.clone.1 | custom fusion | bytes 6561792 | tf_op jit(solution)/shard_map/while/body/eval_jaxpr/jit(_take)/gather | solution.py:64
  310.2 14.9 %copy.110 = bf16[16,128,25,32]{1,0,3,2:T(8,128)(2,1)} copy(bf16[16,128,25,32]{3,2,1,0:T(8,128)(2,1)} %bitcast.209) | data formatting | bytes 6553600 | tf_op jit(solution)/shard_map/while/body/eval_jaxpr/jit(_take)/gather | solution.py:64
  325.1 3.6 fusion.93
  328.7 19.3 %gather_fusion = bf16[2048,25,32]{2,1,0:T(8,128)(2,1)} fusion(bf16[25,32,256]{1,0,2:T(8,128)(2,1)S(1)} %get-tuple-element.572, s32[2048]{0:T(1024)S(1)} %bitcast_clamp_fusion.4), kind=kCustom, calls=%fused_computation.2.clone.clone.1 | custom fusion | bytes 6561792 | tf_op jit(solution)/shard_map/while/body/eval_jaxpr/jit(_take)/gather | solution.py:64
  348.0 14.9 %copy.110 = bf16[16,128,25,32]{1,0,3,2:T(8,128)(2,1)} copy(bf16[16,128,25,32]{3,2,1,0:T(8,128)(2,1)} %bitcast.209) | data formatting | bytes 6553600 | tf_op jit(solution)/shard_map/while/body/eval_jaxpr/jit(_take)/gather | solution.py:64
  362.9 3.6 fusion.93
  366.5 19.3 %gather_fusion = bf16[2048,25,32]{2,1,0:T(8,128)(2,1)} fusion(bf16[25,32,256]{1,0,2:T(8,128)(2,1)S(1)} %get-tuple-element.572, s32[2048]{0:T(1024)S(1)} %bitcast_clamp_fusion.4), kind=kCustom, calls=%fused_computation.2.clone.clone.1 | custom fusion | bytes 6561792 | tf_op jit(solution)/shard_map/while/body/eval_jaxpr/jit(_take)/gather | solution.py:64
  385.8 14.9 %copy.110 = bf16[16,128,25,32]{1,0,3,2:T(8,128)(2,1)} copy(bf16[16,128,25,32]{3,2,1,0:T(8,128)(2,1)} %bitcast.209) | data formatting | bytes 6553600 | tf_op jit(solution)/shard_map/while/body/eval_jaxpr/jit(_take)/gather | solution.py:64
  400.7 3.6 fusion.93
  404.3 19.3 %gather_fusion = bf16[2048,25,32]{2,1,0:T(8,128)(2,1)} fusion(bf16[25,32,256]{1,0,2:T(8,128)(2,1)S(1)} %get-tuple-element.572, s32[2048]{0:T(1024)S(1)} %bitcast_clamp_fusion.4), kind=kCustom, calls=%fused_computation.2.clone.clone.1 | custom fusion | bytes 6561792 | tf_op jit(solution)/shard_map/while/body/eval_jaxpr/jit(_take)/gather | solution.py:64
  423.6 14.9 %copy.110 = bf16[16,128,25,32]{1,0,3,2:T(8,128)(2,1)} copy(bf16[16,128,25,32]{3,2,1,0:T(8,128)(2,1)} %bitcast.209) | data formatting | bytes 6553600 | tf_op jit(solution)/shard_map/while/body/eval_jaxpr/jit(_take)/gather | solution.py:64
  438.5 3.6 fusion.93
  445.9 267.0 %all-reduce.3.cloned.1.call-done = (f32[25,25,64]{1,2,0:T(8,128)}, f32[25,25,64]{1,2,0:T(8,128)}) async-done(((f32[25,25,64]{1,2,0:T(8,128)}, f32[25,25,64]{1,2,0:T(8,128)}), (f32[25,25,64]{1,2,0:T(8,128)}, f32[25,25,64]{1,2,0:T(8,128)})) %all-reduce.3.cloned.1.call-update) | async-done | bytes 320016 | tf_op jit(solution)/shard_map/psum | solution.py:164
  (162 shorter events, 69.4 us)
Async XLA Ops:
  7.2 28.6 %copy-start = (bf16[128,128]{1,0:T(8,128)(2,1)S(1)}, bf16[128,128]{1,0:T(8,128)(2,1)}, u32[]{:S(2)}) copy-start(bf16[128,128]{1,0:T(8,128)(2,1)} %param.32) | copy-start | bytes 98308
  7.2 705.7 %all-reduce.3.cloned.1.call-start = ((), (), s32[]{:S(2)}) async-start(), calls=%async_computation | async-start | bytes 3276800 | tf_op jit(solution)/shard_map/psum | solution.py:164
  8.1 9.2 %copy-start.7 = (bf16[8,25,25]{2,0,1:T(8,128)(2,1)S(1)}, bf16[8,25,25]{2,0,1:T(8,128)(2,1)}, u32[]{:S(2)}) copy-start(bf16[8,25,25]{2,0,1:T(8,128)(2,1)} %param.28) | copy-start | bytes 30004
  10.4 13.0 %copy-start.9 = (bf16[32,1024]{1,0:T(8,128)(2,1)S(1)}, bf16[32,1024]{1,0:T(8,128)(2,1)}, u32[]{:S(2)}) copy-start(bf16[32,1024]{1,0:T(8,128)(2,1)} %param.33) | copy-start | bytes 196612
  10.4 25.5 %copy-start.11 = (f32[25,1024]{1,0:T(8,128)S(1)}, f32[25,1024]{1,0:T(8,128)}, u32[]{:S(2)}) copy-start(f32[25,1024]{1,0:T(8,128)} %param.24) | copy-start | bytes 307204
  11.2 67.6 %collective-permute-start.1 = (bf16[25,32,64]{2,1,0:T(8,128)(2,1)}, bf16[25,32,64]{2,1,0:T(8,128)(2,1)}, u32[]{:S(2)}, u32[]{:S(2)}) collective-permute-start(bf16[25,32,64]{2,1,0:T(8,128)(2,1)} %get-tuple-element.331), channel_id=1, source_target_pairs={{4,0},{8,4},{12,8},{16,12},{20,16},{24,20},{28,24},{32,28},{36,32}... | collective-permute-start | bytes 307208 | tf_op jit(solution)/shard_map/ppermute | solution.py:17
  13.2 65.7 %collective-permute-start = (bf16[25,32,64]{2,1,0:T(8,128)(2,1)}, bf16[25,32,64]{2,1,0:T(8,128)(2,1)}, u32[]{:S(2)}, u32[]{:S(2)}) collective-permute-start(bf16[25,32,64]{2,1,0:T(8,128)(2,1)} %get-tuple-element.330), channel_id=1, source_target_pairs={{0,4},{4,8},{8,12},{12,16},{16,20},{20,24},{24,28},{28,32},{32,36}... | collective-permute-start | bytes 307208 | tf_op jit(solution)/shard_map/ppermute | solution.py:14
  17.7 20.6 %copy-start.8 = (bf16[8,25,25]{2,0,1:T(8,128)(2,1)S(1)}, bf16[8,25,25]{2,0,1:T(8,128)(2,1)}, u32[]{:S(2)}) copy-start(bf16[8,25,25]{2,0,1:T(8,128)(2,1)} %param.29) | copy-start | bytes 30004
  17.7 25.4 %collective-permute-start.3 = (bf16[25,32,8]{0,1,2:T(8,128)(2,1)S(1)}, bf16[25,32,8]{0,1,2:T(8,128)(2,1)S(1)}, u32[]{:S(2)}, u32[]{:S(2)}) collective-permute-start(bf16[25,32,8]{0,1,2:T(8,128)(2,1)S(1)} %get-tuple-element.333), channel_id=1, source_target_pairs={{4,0},{8,4},{12,8},{16,12},{20,16},{24,20},{28,24},{32,28},{36,32}... | collective-permute-start | bytes 38408 | tf_op jit(solution)/shard_map/ppermute | solution.py:17
  21.5 21.6 %collective-permute-start.2 = (bf16[25,32,8]{0,1,2:T(8,128)(2,1)S(1)}, bf16[25,32,8]{0,1,2:T(8,128)(2,1)S(1)}, u32[]{:S(2)}, u32[]{:S(2)}) collective-permute-start(bf16[25,32,8]{0,1,2:T(8,128)(2,1)S(1)} %get-tuple-element.332), channel_id=1, source_target_pairs={{0,4},{4,8},{8,12},{12,16},{16,20},{20,24},{24,28},{28,32},{32,36}... | collective-permute-start | bytes 38408 | tf_op jit(solution)/shard_map/ppermute | solution.py:14
  35.9 3.6 copy-start.4
  36.6 4.6 copy-start.5
  36.6 5.5 copy-start.10
  58.4 0.9 copy-start.6
  62.8 0.9 copy-start.6
  67.1 0.9 copy-start.6
  71.5 0.9 copy-start.6
  78.9 4.3 copy-start.1
  83.2 194.9 %copy-start.12 = (f32[25,1024]{1,0:T(8,128)S(1)}, f32[25,1024]{1,0:T(8,128)}, u32[]{:S(2)}) copy-start(f32[25,1024]{1,0:T(8,128)} %param.24) | copy-start | bytes 307204
  276.8 14.1 %copy-start.2 = (bf16[25,32,128]{2,0,1:T(8,128)(2,1)S(1)}, bf16[25,32,128]{2,0,1:T(8,128)(2,1)}, u32[]{:S(2)}) copy-start(bf16[25,32,128]{2,0,1:T(8,128)(2,1)} %copy.53) | copy-start | bytes 614404
  442.1 2.9 copy-start.3
Sparse Core Ops, SparseCore 0:
  445.1 267.7 all-reduce.2
where the time goes:
time: 726 us; the launch traced here: 724 us
  local copies, waits for them, and re-layouts  352 us (48%)
  waiting for transfers between devices  267 us (37%)
  matrix products  49.3 us (7%)
  blocking collectives  24.6 us (3%)
  between operations  14.3 us (2%)
  starting transfers between devices  10 us (1%)
    gather x32, local copies, waits for them, and re-layouts, pick(): picked = jnp.take(source, position, axis=2)  325 us
    psum x1, waiting for transfers between devices, local(): lax.psum((grad_leaf, grad_coarse), ('cells', 'chan'))  267 us
    dot_general x8, matrix products, translate_advance(): jnp.einsum('okj,jcot->kct', group_ops, picked, preferred_element_type=jnp...  22.9 us
    dot_general x8, matrix products, slot_advance(): jnp.einsum('kct,jcot->kjo', fields, picked, preferred_element_type=jnp.fl...  21.2 us
  transfers between devices with their start and end apart: 5, of which 1 were waited for; matrix products, arithmetic and copies ran while one was open for 6% of the time, Pallas kernels for 0%

commit v1 on v0

--- a/solution.py
+++ b/solution.py
@@ -161,7 +161,7 @@
     ).astype(jnp.bfloat16)
     grad_leaf = slot_gradients(leaf_source, leaf_lists, leaf_first, back_expansion)
     grad_coarse = slot_gradients(coarse_source, coarse_lists, coarse_first, back_far)
-    grad_leaf, grad_coarse = lax.psum((grad_leaf, grad_coarse), ("cells", "chan"))
+    grad_leaf, grad_coarse = lax.psum(lax.psum((grad_leaf, grad_coarse), "cells"), "chan")
     return (refined, grad_leaf, grad_coarse)
 
 

time: 726 us -> 695 us (0.957)
  waiting for transfers between devices: 267 us -> 235 us
    psum x1 -> x2, waiting for transfers between devices: 267 us -> 235 us  [the longest x1 192 us: local(): lax.psum((grad_leaf, grad_coarse), 'cells')]
  transfers between devices with their start and end apart: 5 -> 6, of which waited for: 1 -> 2; matrix products, arithmetic and copies ran while one was open for 6% -> 6% of each run, Pallas kernels for 0% -> 0%
where the time goes in v1:
time: 695 us; the launch traced here: 693 us
  local copies, waits for them, and re-layouts  351 us (51%)
  waiting for transfers between devices  235 us (34%)
  matrix products  49.2 us (7%)
  blocking collectives  24.9 us (4%)
  between operations  14.4 us (2%)
  starting transfers between devices  10.1 us (1%)
    gather x32, local copies, waits for them, and re-layouts, pick(): picked = jnp.take(source, position, axis=2)  325 us
    psum x1, waiting for transfers between devices, local(): lax.psum((grad_leaf, grad_coarse), 'cells')  192 us
    psum x1, waiting for transfers between devices, local(): lax.psum(lax.psum((grad_leaf, grad_coarse), 'cells'), 'chan')  42.9 us
    dot_general x8, matrix products, translate_advance(): jnp.einsum('okj,jcot->kct', group_ops, picked, preferred_element_type=jnp...  22.8 us
    dot_general x8, matrix products, slot_advance(): jnp.einsum('kct,jcot->kjo', fields, picked, preferred_element_type=jnp.fl...  21.2 us
  transfers between devices with their start and end apart: 6, of which 2 were waited for; matrix products, arithmetic and copies ran while one was open for 6% of the time, Pallas kernels for 0%

profile of v1, /device:TPU:2, one launch (start us, length us, event | category | flops | bytes accessed | tf_op | source)
XLA Modules:
  0.0 692.6 jit_solution(2683578691527246035)
XLA Ops:
  17.7 3.8 collective-permute-start.3
  23.5 12.3 %all_gather.7 = bf16[128,1024]{1,0:T(8,128)(2,1)S(1)} all-gather(bf16[32,1024]{1,0:T(8,128)(2,1)S(1)} %copy-done.9), channel_id=1, replica_groups=mesh['cells'=64,'chan'=4] {'chan'}, dimensions={0}, use_global_device_ids=true | all-gather | bytes 327680 | tf_op jit(solution)/shard_map/all_gather | solution.py:152
  43.5 13.1 %while.57 = (s32[]{:T(128)}, f32[25,32,16]{1,0,2:T(8,128)S(1)}, bf16[4,16,25,25]{3,2,1,0:T(8,128)(2,1)S(1)}, s32[4,16,16]{2,1,0:T(8,128)S(1)}, s32[]{:T(128)}, /...) while((s32[]{:T(128)}, f32[25,32,16]{1,0,2:T(8,128)S(1)}, ...), condition=%wide.region_3.6_spmd.clone, body=%wide.region_2.5_spmd.clone.sunk | while | flops 10678787 | bytes 4553847 | solution.py:85
  56.6 17.5 %while.15 = (s32[]{:T(128)}, f32[4,25,25,16]{1,2,3,0:T(8,128)}, s32[4,16,16]{2,1,0:T(8,128)S(1)}, s32[]{:T(128)}, bf16[25,32,32]{1,0,2:T(8,128)(2,1)S(1)}, /*index=5*/bf16[25,32,16]{1,0,2:T(8,128)(2,1)}, s32[]{:T(128)}) while((s32[]{:T(128)}, f32[4,25,25,16]{1,2,3,0:T(8,128)}, s32[4,16,16]{2,1,0:T(8,128)S(1)}, s32[]{:T(128)}, ...), condition=%wide.region_10.13_spmd, body=%wide.region_9.12_spmd.sunk | while | flops 10653186 | bytes 3270785 | solution.py:102
  83.2 193.4 %while.56 = (s32[]{:T(128)}, f32[25,32,128]{2,0,1:T(8,128)}, bf16[4,16,25,25]{3,2,1,0:T(8,128)(2,1)}, s32[4,16,128]{2,1,0:T(8,128)S(1)}, s32[]{:T(128)}, /*index...) while((s32[]{:T(128)}, f32[25,32,128]{2,0,1:T(8,128)}, bf16[4,16,25,25]{3,2,1,0:T(8,128)(2,1)}, ...), condition=%wide.region_1.3_spmd.clone, body=%wide.region_0.2_spmd.clone.sunk | while | flops 90349568 | bytes 18425984 | solution.py:85
  83.2 19.3 %gather_fusion.2 = bf16[2048,25,32]{2,1,0:T(8,128)(2,1)} fusion(bf16[25,32,256]{1,0,2:T(8,128)(2,1)S(1)} %get-tuple-element.529, s32[2048]{0:T(1024)S(1)} %bitcast_clamp_fusion.5), kind=kCustom, calls=%fused_computation.clone.clone.1 | custom fusion | bytes 6561792 | tf_op jit(solution)/shard_map/while/body/eval_jaxpr/jit(_take)/gather | solution.py:64
  102.5 24.5 %copy.113 = bf16[16,128,25,32]{1,2,0,3:T(8,128)(2,1)} copy(bf16[16,128,25,32]{3,2,1,0:T(8,128)(2,1)} %bitcast.208) | data formatting | bytes 6553600 | tf_op jit(solution)/shard_map/while/body/eval_jaxpr/jit(_take)/gather | solution.py:64
  127.0 4.5 fusion.98
  131.5 19.3 %gather_fusion.2 = bf16[2048,25,32]{2,1,0:T(8,128)(2,1)} fusion(bf16[25,32,256]{1,0,2:T(8,128)(2,1)S(1)} %get-tuple-element.529, s32[2048]{0:T(1024)S(1)} %bitcast_clamp_fusion.5), kind=kCustom, calls=%fused_computation.clone.clone.1 | custom fusion | bytes 6561792 | tf_op jit(solution)/shard_map/while/body/eval_jaxpr/jit(_take)/gather | solution.py:64
  150.8 24.5 %copy.113 = bf16[16,128,25,32]{1,2,0,3:T(8,128)(2,1)} copy(bf16[16,128,25,32]{3,2,1,0:T(8,128)(2,1)} %bitcast.208) | data formatting | bytes 6553600 | tf_op jit(solution)/shard_map/while/body/eval_jaxpr/jit(_take)/gather | solution.py:64
  175.3 4.6 fusion.98
  179.9 19.3 %gather_fusion.2 = bf16[2048,25,32]{2,1,0:T(8,128)(2,1)} fusion(bf16[25,32,256]{1,0,2:T(8,128)(2,1)S(1)} %get-tuple-element.529, s32[2048]{0:T(1024)S(1)} %bitcast_clamp_fusion.5), kind=kCustom, calls=%fused_computation.clone.clone.1 | custom fusion | bytes 6561792 | tf_op jit(solution)/shard_map/while/body/eval_jaxpr/jit(_take)/gather | solution.py:64
  199.1 24.5 %copy.113 = bf16[16,128,25,32]{1,2,0,3:T(8,128)(2,1)} copy(bf16[16,128,25,32]{3,2,1,0:T(8,128)(2,1)} %bitcast.208) | data formatting | bytes 6553600 | tf_op jit(solution)/shard_map/while/body/eval_jaxpr/jit(_take)/gather | solution.py:64
  223.7 4.6 fusion.98
  228.3 19.3 %gather_fusion.2 = bf16[2048,25,32]{2,1,0:T(8,128)(2,1)} fusion(bf16[25,32,256]{1,0,2:T(8,128)(2,1)S(1)} %get-tuple-element.529, s32[2048]{0:T(1024)S(1)} %bitcast_clamp_fusion.5), kind=kCustom, calls=%fused_computation.clone.clone.1 | custom fusion | bytes 6561792 | tf_op jit(solution)/shard_map/while/body/eval_jaxpr/jit(_take)/gather | solution.py:64
  247.5 24.5 %copy.113 = bf16[16,128,25,32]{1,2,0,3:T(8,128)(2,1)} copy(bf16[16,128,25,32]{3,2,1,0:T(8,128)(2,1)} %bitcast.208) | data formatting | bytes 6553600 | tf_op jit(solution)/shard_map/while/body/eval_jaxpr/jit(_take)/gather | solution.py:64
  272.1 4.6 fusion.98
  276.6 151.0 %while.14 = (s32[]{:T(128)}, f32[4,25,25,16]{1,3,2,0:T(8,128)}, s32[4,16,128]{2,1,0:T(8,128)S(1)}, s32[]{:T(128)}, bf16[25,32,256]{1,0,2:T(8,128)(2,1)S(1)}, /*index=5*/bf16[25,32,128]{2,0,1:T(8,128)(2,1)S(1)}, s32[]{:T(128)}) while((s32[]{:T(128)}, f32[4,25,25,16]{1,3,2,0:T(8,128)}, s32[4,16,128]{2,1,0:T(8,128)S(1)}, s32[]{:T(128)}, ...), condition=%wide.region_6.9_spmd, body=%wide.region_5.8_spmd.sunk | while | flops 85229568 | bytes 16853100 | solution.py:102
  276.7 19.3 %gather_fusion = bf16[2048,25,32]{2,1,0:T(8,128)(2,1)} fusion(bf16[25,32,256]{1,0,2:T(8,128)(2,1)S(1)} %get-tuple-element.574, s32[2048]{0:T(1024)S(1)} %bitcast_clamp_fusion.4), kind=kCustom, calls=%fused_computation.2.clone.clone.1 | custom fusion | bytes 6561792 | tf_op jit(solution)/shard_map/while/body/eval_jaxpr/jit(_take)/gather | solution.py:64
  295.9 14.9 %copy.110 = bf16[16,128,25,32]{1,0,3,2:T(8,128)(2,1)} copy(bf16[16,128,25,32]{3,2,1,0:T(8,128)(2,1)} %bitcast.209) | data formatting | bytes 6553600 | tf_op jit(solution)/shard_map/while/body/eval_jaxpr/jit(_take)/gather | solution.py:64
  310.8 3.6 fusion.93
  314.4 19.3 %gather_fusion = bf16[2048,25,32]{2,1,0:T(8,128)(2,1)} fusion(bf16[25,32,256]{1,0,2:T(8,128)(2,1)S(1)} %get-tuple-element.574, s32[2048]{0:T(1024)S(1)} %bitcast_clamp_fusion.4), kind=kCustom, calls=%fused_computation.2.clone.clone.1 | custom fusion | bytes 6561792 | tf_op jit(solution)/shard_map/while/body/eval_jaxpr/jit(_take)/gather | solution.py:64
  333.7 14.9 %copy.110 = bf16[16,128,25,32]{1,0,3,2:T(8,128)(2,1)} copy(bf16[16,128,25,32]{3,2,1,0:T(8,128)(2,1)} %bitcast.209) | data formatting | bytes 6553600 | tf_op jit(solution)/shard_map/while/body/eval_jaxpr/jit(_take)/gather | solution.py:64
  348.5 3.6 fusion.93
  352.2 19.3 %gather_fusion = bf16[2048,25,32]{2,1,0:T(8,128)(2,1)} fusion(bf16[25,32,256]{1,0,2:T(8,128)(2,1)S(1)} %get-tuple-element.574, s32[2048]{0:T(1024)S(1)} %bitcast_clamp_fusion.4), kind=kCustom, calls=%fused_computation.2.clone.clone.1 | custom fusion | bytes 6561792 | tf_op jit(solution)/shard_map/while/body/eval_jaxpr/jit(_take)/gather | solution.py:64
  371.4 14.9 %copy.110 = bf16[16,128,25,32]{1,0,3,2:T(8,128)(2,1)} copy(bf16[16,128,25,32]{3,2,1,0:T(8,128)(2,1)} %bitcast.209) | data formatting | bytes 6553600 | tf_op jit(solution)/shard_map/while/body/eval_jaxpr/jit(_take)/gather | solution.py:64
  386.3 3.6 fusion.93
  389.9 19.3 %gather_fusion = bf16[2048,25,32]{2,1,0:T(8,128)(2,1)} fusion(bf16[25,32,256]{1,0,2:T(8,128)(2,1)S(1)} %get-tuple-element.574, s32[2048]{0:T(1024)S(1)} %bitcast_clamp_fusion.4), kind=kCustom, calls=%fused_computation.2.clone.clone.1 | custom fusion | bytes 6561792 | tf_op jit(solution)/shard_map/while/body/eval_jaxpr/jit(_take)/gather | solution.py:64
  409.2 14.9 %copy.110 = bf16[16,128,25,32]{1,0,3,2:T(8,128)(2,1)} copy(bf16[16,128,25,32]{3,2,1,0:T(8,128)(2,1)} %bitcast.209) | data formatting | bytes 6553600 | tf_op jit(solution)/shard_map/while/body/eval_jaxpr/jit(_take)/gather | solution.py:64
  432.4 192.5 %all-reduce.5.cloned.1.call-done = (f32[25,25,64]{1,2,0:T(8,128)}, f32[25,25,64]{1,2,0:T(8,128)}) async-done(((f32[25,25,64]{1,2,0:T(8,128)}, f32[25,25,64]{1,2,0:T(8,128)}), (f32[25,25,64]{1,2,0:T(8,128)}, f32[25,25,64]{1,2,0:T(8,128)})) %all-reduce.5.cloned.1.call-update) | async-done | bytes 320016 | tf_op jit(solution)/shard_map/psum | solution.py:164
  624.9 12.6 %all_gather.6 = bf16[128,1024]{1,0:T(8,128)(2,1)S(1)} all-gather(bf16[32,1024]{1,0:T(8,128)(2,1)S(1)} %multiply_reduce_fusion), channel_id=1, replica_groups=mesh['cells'=64,'chan'=4] {'chan'}, dimensions={0}, use_global_device_ids=true | all-gather | bytes 327680 | tf_op jit(solution)/shard_map/all_gather | solution.py:146
  638.4 42.9 %all-reduce.7.cloned.1.call-done = (f32[25,25,64]{1,2,0:T(8,128)}, f32[25,25,64]{1,2,0:T(8,128)}) async-done(((f32[25,25,64]{1,2,0:T(8,128)}, f32[25,25,64]{1,2,0:T(8,128)}), (f32[25,25,64]{1,2,0:T(8,128)}, f32[25,25,64]{1,2,0:T(8,128)})) %all-reduce.7.cloned.1.call-update) | async-done | bytes 320016 | tf_op jit(solution)/shard_map/psum | solution.py:164
  (169 shorter events, 73.0 us)
Async XLA Ops:
  7.2 28.6 %copy-start = (bf16[128,128]{1,0:T(8,128)(2,1)S(1)}, bf16[128,128]{1,0:T(8,128)(2,1)}, u32[]{:S(2)}) copy-start(bf16[128,128]{1,0:T(8,128)(2,1)} %param.32) | copy-start | bytes 98308
  7.2 617.7 %all-reduce.5.cloned.1.call-start = ((), (), s32[]{:S(2)}) async-start(), calls=%async_computation | async-start | bytes 3276800 | tf_op jit(solution)/shard_map/psum | solution.py:164
  8.1 9.2 %copy-start.7 = (bf16[8,25,25]{2,0,1:T(8,128)(2,1)S(1)}, bf16[8,25,25]{2,0,1:T(8,128)(2,1)}, u32[]{:S(2)}) copy-start(bf16[8,25,25]{2,0,1:T(8,128)(2,1)} %param.28) | copy-start | bytes 30004
  8.8 27.1 %copy-start.11 = (s32[1024]{0:T(1024)}, s32[1024]{0:T(1024)S(1)}, u32[]{:S(2)}) copy-start(s32[1024]{0:T(1024)S(1)} %broadcast_subtract_fusion) | copy-start | bytes 12292
  10.4 13.0 %copy-start.9 = (bf16[32,1024]{1,0:T(8,128)(2,1)S(1)}, bf16[32,1024]{1,0:T(8,128)(2,1)}, u32[]{:S(2)}) copy-start(bf16[32,1024]{1,0:T(8,128)(2,1)} %param.33) | copy-start | bytes 196612
  10.4 25.5 %copy-start.13 = (f32[25,1024]{1,0:T(8,128)S(1)}, f32[25,1024]{1,0:T(8,128)}, u32[]{:S(2)}) copy-start(f32[25,1024]{1,0:T(8,128)} %param.24) | copy-start | bytes 307204
  11.3 67.6 %collective-permute-start.1 = (bf16[25,32,64]{2,1,0:T(8,128)(2,1)}, bf16[25,32,64]{2,1,0:T(8,128)(2,1)}, u32[]{:S(2)}, u32[]{:S(2)}) collective-permute-start(bf16[25,32,64]{2,1,0:T(8,128)(2,1)} %get-tuple-element.333), channel_id=1, source_target_pairs={{4,0},{8,4},{12,8},{16,12},{20,16},{24,20},{28,24},{32,28},{36,32}... | collective-permute-start | bytes 307208 | tf_op jit(solution)/shard_map/ppermute | solution.py:17
  13.2 65.7 %collective-permute-start = (bf16[25,32,64]{2,1,0:T(8,128)(2,1)}, bf16[25,32,64]{2,1,0:T(8,128)(2,1)}, u32[]{:S(2)}, u32[]{:S(2)}) collective-permute-start(bf16[25,32,64]{2,1,0:T(8,128)(2,1)} %get-tuple-element.332), channel_id=1, source_target_pairs={{0,4},{4,8},{8,12},{12,16},{16,20},{20,24},{24,28},{28,32},{32,36}... | collective-permute-start | bytes 307208 | tf_op jit(solution)/shard_map/ppermute | solution.py:14
  17.7 20.7 %copy-start.8 = (bf16[8,25,25]{2,0,1:T(8,128)(2,1)S(1)}, bf16[8,25,25]{2,0,1:T(8,128)(2,1)}, u32[]{:S(2)}) copy-start(bf16[8,25,25]{2,0,1:T(8,128)(2,1)} %param.29) | copy-start | bytes 30004
  17.7 25.4 %collective-permute-start.3 = (bf16[25,32,8]{0,1,2:T(8,128)(2,1)S(1)}, bf16[25,32,8]{0,1,2:T(8,128)(2,1)S(1)}, u32[]{:S(2)}, u32[]{:S(2)}) collective-permute-start(bf16[25,32,8]{0,1,2:T(8,128)(2,1)S(1)} %get-tuple-element.335), channel_id=1, source_target_pairs={{4,0},{8,4},{12,8},{16,12},{20,16},{24,20},{28,24},{32,28},{36,32}... | collective-permute-start | bytes 38408 | tf_op jit(solution)/shard_map/ppermute | solution.py:17
  21.5 21.6 %collective-permute-start.2 = (bf16[25,32,8]{0,1,2:T(8,128)(2,1)S(1)}, bf16[25,32,8]{0,1,2:T(8,128)(2,1)S(1)}, u32[]{:S(2)}, u32[]{:S(2)}) collective-permute-start(bf16[25,32,8]{0,1,2:T(8,128)(2,1)S(1)} %get-tuple-element.334), channel_id=1, source_target_pairs={{0,4},{4,8},{8,12},{12,16},{16,20},{20,24},{24,28},{28,32},{32,36}... | collective-permute-start | bytes 38408 | tf_op jit(solution)/shard_map/ppermute | solution.py:14
  35.9 3.6 copy-start.4
  36.6 4.6 copy-start.5
  36.7 5.5 copy-start.10
  58.4 0.9 copy-start.6
  62.8 0.9 copy-start.6
  67.2 0.9 copy-start.6
  71.5 0.9 copy-start.6
  78.9 4.3 copy-start.1
  83.2 193.5 %copy-start.2 = (bf16[25,32,128]{2,0,1:T(8,128)(2,1)S(1)}, bf16[25,32,128]{2,0,1:T(8,128)(2,1)}, u32[]{:S(2)}) copy-start(bf16[25,32,128]{2,0,1:T(8,128)(2,1)} %copy.53) | copy-start | bytes 614404
  427.6 4.1 copy-start.12
  427.6 4.1 copy-start.14
  431.7 205.8 %copy-start.3 = (bf16[32,1024]{1,0:T(8,128)(2,1)S(1)}, bf16[32,1024]{1,0:T(8,128)(2,1)}, u32[]{:S(2)}) copy-start(bf16[32,1024]{1,0:T(8,128)(2,1)} %param.23) | copy-start | bytes 196612
  431.7 249.6 %all-reduce.7.cloned.1.call-start = ((), (), s32[]{:S(2)}) async-start(), calls=%async_computation.1 | async-start | bytes 3276800 | tf_op jit(solution)/shard_map/psum | solution.py:164
Sparse Core Ops, SparseCore 0:
  431.8 193.0 all-reduce.4
  627.3 53.9 all-reduce.6
